TPU v7x, 128 devices: a whole 4x4x4 slice. The times are simulated.
128 devices in a mesh: ctx: 32 (over x, z, y_lo), fsdp: 4 (over y_hi, core).
Axes of the slice: x: 4, y: 4 (y_hi: 2, y_lo: 2; y = y_hi * 2 + y_lo), z: 4, core: 2. Of those that a mesh axis runs over, the one named last changes fastest.
Arguments:
- x_cur: bfloat16 [4, 8192, 2048], P('fsdp', 'ctx'), may hold values from -6 to 6
- x_next: bfloat16 [4, 8192, 2048], P('fsdp', 'ctx'), may hold values from -6 to 6
- cot_cur: bfloat16 [4, 8192, 2048], P('fsdp', 'ctx'), may hold values from -6 to 6
- cot_next: bfloat16 [4, 8192, 2048], P('fsdp', 'ctx'), may hold values from -6 to 6
- w_q: bfloat16 [2048, 1024], P('fsdp')
- w_kv: bfloat16 [2048, 512], P('fsdp')
- w_out: bfloat16 [2048, 1024], P('fsdp'), may hold values from -0.1875 to 0.1875
Outputs:
- x_prev: bfloat16 [4, 8192, 2048], P('fsdp', 'ctx')
- grad_cur: bfloat16 [4, 8192, 2048], P('fsdp', 'ctx')
- grad_weights: float32 [2048, 2560], P(('ctx', 'fsdp'))
All inputs are finite; a program needn't handle non-finite values.
Results may differ from a plain program's by a relative error of at most 0.015.
The roundings to bfloat16 on the way count: a program that leaves them out, or rounds other values in their place, can miss the bound.
Values may be sent and summed in bfloat16 or wider, within the bound.
No kernel may reach another device: no remote copies, remote signals or barrier semaphores. Data moves between devices by JAX's collectives and lax.ppermute only.
A program may use at most 192 MiB of HBM per device.

v0:
```python
import math
import jax
import jax.numpy as jnp
from jax import lax
from jax.sharding import Mesh
from jax.sharding import PartitionSpec as P

QUERY_HEADS = 8
KEY_VALUE_HEADS = 2
HEAD_SIZE = 128
WINDOW_TOKENS = 1024
EPS = 1e-05
CTX = ("x", "z", "yl")
FSDP = ("yh", "c")
CHIPS = ("x", "z", "yl", "yh")


def from_behind(value, axis, steps):
    count = lax.axis_size(axis)
    leading, last = (max(0, -steps), min(count, count - steps))
    return lax.ppermute(value, axis, [(source, source + steps) for source in range(leading, last)])


def swap_cores(value):
    return lax.ppermute(value, "c", [(0, 1), (1, 0)])


def normalize(rows):
    values = rows.astype(jnp.float32)
    inv_rms = lax.rsqrt(jnp.mean(values * values, axis=-1, keepdims=True) + EPS)
    return (values * inv_rms, inv_rms)


def head_block(items, allowed):
    quer3, keys2, vals2, grad3 = items
    scale = 1.0 / math.sqrt(HEAD_SIZE)
    scores = jnp.einsum("imd,jd->mij", quer3, keys2, preferred_element_type=jnp.float32) * scale
    scores = jnp.where(allowed[None], scores, -jnp.inf)
    top = jnp.max(scores, axis=-1, keepdims=True)
    expo = jnp.exp(scores - top)
    probs = expo / jnp.sum(expo, axis=-1, keepdims=True)
    probs_low = probs.astype(jnp.bfloat16)
    attended = jnp.einsum("mij,jd->imd", probs_low, vals2, preferred_element_type=jnp.float32)
    grad_probs = jnp.einsum("imd,jd->mij", grad3, vals2, preferred_element_type=jnp.float32)
    delta = jnp.einsum("imd,imd->mi", grad3.astype(jnp.float32), attended)
    grad_scores = (probs * (grad_probs - delta[..., None]) * scale).astype(jnp.bfloat16)
    grad_query = jnp.einsum("mij,jd->imd", grad_scores, keys2, preferred_element_type=jnp.float32)
    key_gradient = jnp.einsum("mij,imd->jd", grad_scores, quer3, preferred_element_type=jnp.float32)
    value_gradient = jnp.einsum("mij,imd->jd", probs_low, grad3, preferred_element_type=jnp.float32)
    return (
        attended.astype(jnp.bfloat16),
        grad_query.astype(jnp.bfloat16),
        key_gradient.astype(jnp.bfloat16),
        value_gradient.astype(jnp.bfloat16),
    )


def window_block(query_rows, key_value_pairs, output_gradient, base):
    window_extent = key_value_pairs.shape[0]
    element_count = query_rows.shape[0]
    query_group = QUERY_HEADS // KEY_VALUE_HEADS
    query_pos = base + jnp.arange(element_count, dtype=jnp.int32)
    key_pos = base - WINDOW_TOKENS + jnp.arange(window_extent, dtype=jnp.int32)
    offset = query_pos[:, None] - key_pos[None, :]
    allowed = (offset >= 0) & (offset < WINDOW_TOKENS) & (key_pos[None, :] >= 0)
    query_grouped = query_rows.reshape(
        element_count, KEY_VALUE_HEADS, query_group, HEAD_SIZE
    ).transpose(1, 0, 2, 3)
    gradient_grouped = output_gradient.reshape(
        element_count, KEY_VALUE_HEADS, query_group, HEAD_SIZE
    ).transpose(1, 0, 2, 3)
    key_tensor = (
        key_value_pairs[:, : KEY_VALUE_HEADS * HEAD_SIZE]
        .reshape(window_extent, KEY_VALUE_HEADS, HEAD_SIZE)
        .transpose(1, 0, 2)
    )
    value_tensor = (
        key_value_pairs[:, KEY_VALUE_HEADS * HEAD_SIZE :]
        .reshape(window_extent, KEY_VALUE_HEADS, HEAD_SIZE)
        .transpose(1, 0, 2)
    )

    def per_head(items):
        return head_block(items, allowed)

    attended, grad_query, key_gradient, value_gradient = lax.map(
        per_head, (query_grouped, key_tensor, value_tensor, gradient_grouped)
    )
    attended = attended.transpose(1, 0, 2, 3).reshape(element_count, QUERY_HEADS * HEAD_SIZE)
    grad_query = grad_query.transpose(1, 0, 2, 3).reshape(element_count, QUERY_HEADS * HEAD_SIZE)
    key_gradient = key_gradient.transpose(1, 0, 2).reshape(
        window_extent, KEY_VALUE_HEADS * HEAD_SIZE
    )
    value_gradient = value_gradient.transpose(1, 0, 2).reshape(
        window_extent, KEY_VALUE_HEADS * HEAD_SIZE
    )
    value_partial_sum = jnp.concatenate([key_gradient, value_gradient], 1)
    return (attended, grad_query, value_partial_sum)


def shards(x_cur, x_next, cot_cur, cot_next, w_q, w_kv, w_out):
    full_q, full_kv, full_out = (
        lax.all_gather(w_q, FSDP, axis=0, tiled=True),
        lax.all_gather(w_kv, FSDP, axis=0, tiled=True),
        lax.all_gather(w_out, FSDP, axis=0, tiled=True),
    )
    seq_count, shard, width = x_cur.shape
    base = lax.axis_index(CTX) * shard
    preds = WINDOW_TOKENS // shard
    normed, inv_rms = normalize(x_cur)
    hidden = normed.astype(jnp.bfloat16)
    query_rows = jnp.einsum(
        "sid,dc->sic", hidden, full_q, preferred_element_type=jnp.float32
    ).astype(jnp.bfloat16)
    key_value_pairs = jnp.einsum(
        "sid,dc->sic", hidden, full_kv, preferred_element_type=jnp.float32
    ).astype(jnp.bfloat16)
    grad_attn = (
        2.0 * jnp.einsum("sid,dc->sic", cot_next, full_out, preferred_element_type=jnp.float32)
    ).astype(jnp.bfloat16)
    earlier = []
    for hop in range(1, preds + 1):
        earlier.append(from_behind(key_value_pairs, CTX, hop))
    window_keys = jnp.concatenate(earlier[::-1] + [key_value_pairs], axis=1)

    def per_sequence(items):
        q_rows, kv_rows, g_rows = items
        return window_block(q_rows, kv_rows, g_rows, base)

    attended, grad_query, value_partial_sum = lax.map(
        per_sequence, (query_rows, window_keys, grad_attn)
    )
    owned = value_partial_sum[:, WINDOW_TOKENS:].astype(jnp.float32)
    for hop in range(1, preds + 1):
        piece = value_partial_sum[
            :, WINDOW_TOKENS - hop * shard : WINDOW_TOKENS - (hop - 1) * shard
        ]
        owned = owned + from_behind(piece, CTX, -hop).astype(jnp.float32)
    grad_kv = owned.astype(jnp.bfloat16)
    layer_out = jnp.einsum("sic,dc->sid", attended, full_out, preferred_element_type=jnp.float32)
    x_prev = (x_next.astype(jnp.float32) - 2.0 * layer_out).astype(jnp.bfloat16)
    grad_hidden = jnp.einsum("sic,dc->sid", grad_query, full_q, preferred_element_type=jnp.float32)
    grad_hidden = grad_hidden + jnp.einsum(
        "sic,dc->sid", grad_kv, full_kv, preferred_element_type=jnp.float32
    )
    grad_x = inv_rms * (
        grad_hidden - normed * jnp.mean(grad_hidden * normed, axis=-1, keepdims=True)
    )
    grad_cur = (cot_cur.astype(jnp.float32) + grad_x).astype(jnp.bfloat16)
    core = lax.axis_index("c")
    token_total = seq_count * shard * lax.axis_size(CTX) * lax.axis_size(FSDP)
    rows_in = hidden.reshape(seq_count * shard, width)
    rows_out = cot_next.reshape(seq_count * shard, width)
    both_in = jnp.concatenate([rows_in, swap_cores(rows_in)], axis=0)
    both_out = jnp.concatenate([rows_out, swap_cores(rows_out)], axis=0)

    def halves(rows):
        rows = rows.reshape(seq_count * shard, -1)
        half = rows.shape[1] // 2
        first = core == 0
        return (
            jnp.where(first, rows[:, :half], rows[:, half:]),
            jnp.where(first, rows[:, half:], rows[:, :half]),
        )

    kept, sent = zip(halves(grad_query), halves(grad_kv), halves(attended))
    kept = jnp.concatenate(kept, axis=1)
    arrived = swap_cores(jnp.concatenate(sent, axis=1))
    split = grad_query.shape[-1] // 2 + grad_kv.shape[-1] // 2
    left = jnp.concatenate([kept, arrived], axis=0)
    contract_rows = (((0,), (0,)), ((), ()))
    term_in = lax.dot_general(
        both_in, left[:, :split], contract_rows, preferred_element_type=jnp.float32
    )
    term_out = 2.0 * lax.dot_general(
        both_out, left[:, split:], contract_rows, preferred_element_type=jnp.float32
    )
    terms = jnp.concatenate([term_in, term_out], axis=1).astype(jnp.bfloat16)
    chips = lax.axis_size(CHIPS)
    terms = terms.reshape(chips, width // chips, -1)
    terms = lax.all_to_all(terms, CHIPS, 0, 0)
    summed = jnp.sum(terms.astype(jnp.float32), axis=0) * (1.0 / math.sqrt(token_total))
    mine = summed.shape[0] // 2
    upper = jnp.where(core == 0, summed[:mine], summed[mine:])
    lower = swap_cores(jnp.where(core == 0, summed[mine:], summed[:mine]))
    zero = jnp.where(core == 0, upper, lower)
    one = jnp.where(core == 0, lower, upper)
    q_half = grad_query.shape[-1] // 2
    grad_weights = jnp.concatenate(
        [
            zero[:, :q_half],
            one[:, :q_half],
            zero[:, q_half:split],
            one[:, q_half:split],
            zero[:, split:],
            one[:, split:],
        ],
        axis=1,
    )
    return (x_prev, grad_cur, grad_weights)


def solution(mesh):
    mesh = Mesh(mesh.devices.reshape(4, 4, 2, 2, 2), CTX + FSDP)
    in_specs = (
        P(FSDP, CTX, None),
        P(FSDP, CTX, None),
        P(FSDP, CTX, None),
        P(FSDP, CTX, None),
        P(FSDP, None),
        P(FSDP, None),
        P(FSDP, None),
    )
    out_specs = (P(FSDP, CTX, None), P(FSDP, CTX, None), P(CTX + FSDP, None))
    return jax.shard_map(shards, mesh=mesh, in_specs=in_specs, out_specs=out_specs, check_vma=False)
```

profile of v0, /device:TPU:71, one launch (start us, length us, event | category | flops | bytes accessed | tf_op | source)
XLA Modules:
  0.0 315.3 jit_solution(6684000862140531037)
XLA Ops:
  7.2 0.7 all-gather.4.cloned.1.call-update
  8.0 0.7 all-gather.8.cloned.1.call-update
  8.7 0.7 all-gather.6.cloned.1.call-update
  9.4 0.8 collective-permute-start.10
  10.7 27.6 %all-gather.4.cloned.1.call-done = bf16[2048,512]{1,0:T(8,128)(2,1)} async-done(((bf16[512,512]{1,0:T(8,128)(2,1)}), bf16[2048,512]{1,0:T(8,128)(2,1)}) %all-gather.4.cloned.1.call-update) | async-done | bytes 2097168 | tf_op jit(solution)/shard_map/all_gather | solution.py:104
  38.3 2.3 fusion.77
  40.6 1.3 collective-permute-start
  41.9 2.9 collective-permute-start.1
  44.8 1.9 collective-permute-start.2
  46.8 1.9 collective-permute-start.3
  48.7 9.1 %collective-permute-done = bf16[1,256,512]{2,1,0:T(8,128)(2,1)S(1)} collective-permute-done((bf16[1,256,512]{2,1,0:T(8,128)(2,1)S(1)}, bf16[1,256,512]{2,1,0:T(8,128)(2,1)S(1)}, u32[]{:S(2)}, u32[]{:S(2)}) %collective-permute-start) | collective-permute-done | bytes 262176 | tf_op jit(solution)/shard_map/ppermute | solution.py:21
  57.9 11.3 %collective-permute-done.2 = bf16[1,256,512]{2,1,0:T(8,128)(2,1)S(1)} collective-permute-done((bf16[1,256,512]{2,1,0:T(8,128)(2,1)S(1)}, bf16[1,256,512]{2,1,0:T(8,128)(2,1)S(1)}, u32[]{:S(2)}, u32[]{:S(2)}) %collective-permute-start.2) | collective-permute-done | bytes 262176 | tf_op jit(solution)/shard_map/ppermute | solution.py:21
  69.4 0.9 copy.49
  70.3 1.1 copy.38
  71.4 14.4 %all-gather.8.cloned.1.call-done = bf16[2048,1024]{1,0:T(8,128)(2,1)} async-done(((bf16[512,1024]{1,0:T(8,128)(2,1)}), bf16[2048,1024]{1,0:T(8,128)(2,1)}) %all-gather.8.cloned.1.call-update) | async-done | bytes 4194320 | tf_op jit(solution)/shard_map/all_gather | solution.py:105
  85.8 3.8 %fusion.76 = bf16[256,1024]{1,0:T(8,128)(2,1)S(1)} fusion(bf16[2048,1024]{1,0:T(8,128)(2,1)} %all-gather.8.cloned.1.call-done, bf16[1,256,2048]{2,1,0:T(8,128)(2,1)} %param.12), kind=kOutput, calls=%fused_computation.93 | convolution fusion | flops 1074266112 | bytes 5767168 | tf_op jit(solution)/shard_map/sid,dc->sic/dot_general | solution.py:119
  89.6 0.4 reshape.125
  90.0 37.9 %all-gather.6.cloned.1.call-done = bf16[2048,1024]{1,0:T(8,128)(2,1)} async-done(((bf16[512,1024]{1,0:T(8,128)(2,1)}), bf16[2048,1024]{1,0:T(8,128)(2,1)}) %all-gather.6.cloned.1.call-update) | async-done | bytes 4194320 | tf_op jit(solution)/shard_map/all_gather | solution.py:103
  127.9 3.4 %convolution_convert_fusion.2 = bf16[256,1024]{1,0:T(8,128)(2,1)S(1)} fusion(bf16[256,2048]{1,0:T(8,128)(2,1)S(1)} %fusion.78, bf16[2048,1024]{1,0:T(8,128)(2,1)} %all-gather.6.cloned.1.call-done), kind=kOutput, calls=%fused_computation.94 | convolution fusion | flops 1074003968 | bytes 5767168 | tf_op jit(solution)/shard_map/sid,dc->sic/dot_general | solution.py:112
  131.7 1.2 copy_bitcast_fusion
  132.9 46.7 %while.29 = (s32[]{:T(128)}, bf16[2,256,4,128]{1,3,2,0:T(8,128)(2,1)}, bf16[2,256,4,128]{1,3,2,0:T(8,128)(2,1)}, bf16[2,1280,128]{1,2,0:T(8,128)(2,1)}, bf16[2,1...) while((s32[]{:T(128)}, ...), condition=%wide.region_4.5_spmd.clone, body=%wide.region_1.4_spmd.clone.sunk | while | flops 2030305536 | bytes 57441732 | solution.py:86
  132.9 0.9 fusion.142
  133.8 1.0 bitcast_convert_fusion.3
  135.0 5.2 %exponential_reduce_fusion.2 = (f32[4,256]{1,0:T(4,128)S(1)}, f32[4,256,1280]{1,2,0:T(8,128)}) fusion(pred[256,1280]{0,1:T(8,128)(4,1)S(1)} %fusion.142, bf16[2,1280,128]{2,1,0:T(8,128)(2,1)} %get-tuple-element.280, s32[]{:T(128)S(6)} %copy.69, bf16[2,256,4,128]{3,1,2,0:T(8,128)(2,1)} %get-tuple-element.281), kind=kOutput, calls=%fused_computation.9.clone.1 | convolution fusion | flops 340788480 | bytes 6165504 | tf_op jit(solution)/shard_map/while/body/eval_jaxpr/while/body/eval_jaxpr/sub | solution.py:40
  140.2 4.0 %fusion.143 = bf16[4,256,1280]{1,2,0:T(8,128)(2,1)S(1)} fusion(f32[4,256]{1,0:T(4,128)S(1)} %get-tuple-element.242, f32[4,256,1280]{1,2,0:T(8,128)} %get-tuple-element.243), kind=kLoop, calls=%fused_computation.18.clone.1 | loop fusion | flops 2621440 | bytes 7868416 | tf_op jit(solution)/shard_map/while/body/eval_jaxpr/while/body/eval_jaxpr/convert_element_type | solution.py:42
  144.2 1.9 fusion.148
  146.1 2.2 fusion.144
  148.4 2.5 fusion.146
  151.1 1.8 fusion.149
  152.9 2.2 fusion.147
  155.4 0.9 constant_dynamic-update-slice_fusion.10
  156.2 0.9 fusion.142
  157.2 1.0 bitcast_convert_fusion.3
  158.4 5.2 %exponential_reduce_fusion.2 = (f32[4,256]{1,0:T(4,128)S(1)}, f32[4,256,1280]{1,2,0:T(8,128)}) fusion(pred[256,1280]{0,1:T(8,128)(4,1)S(1)} %fusion.142, bf16[2,1280,128]{2,1,0:T(8,128)(2,1)} %get-tuple-element.280, s32[]{:T(128)S(6)} %copy.69, bf16[2,256,4,128]{3,1,2,0:T(8,128)(2,1)} %get-tuple-element.281), kind=kOutput, calls=%fused_computation.9.clone.1 | convolution fusion | flops 340788480 | bytes 6165504 | tf_op jit(solution)/shard_map/while/body/eval_jaxpr/while/body/eval_jaxpr/sub | solution.py:40
  163.6 4.0 %fusion.143 = bf16[4,256,1280]{1,2,0:T(8,128)(2,1)S(1)} fusion(f32[4,256]{1,0:T(4,128)S(1)} %get-tuple-element.242, f32[4,256,1280]{1,2,0:T(8,128)} %get-tuple-element.243), kind=kLoop, calls=%fused_computation.18.clone.1 | loop fusion | flops 2621440 | bytes 7868416 | tf_op jit(solution)/shard_map/while/body/eval_jaxpr/while/body/eval_jaxpr/convert_element_type | solution.py:42
  167.6 1.9 fusion.148
  169.4 2.2 fusion.144
  171.8 2.5 fusion.146
  174.5 1.8 fusion.149
  176.3 2.3 fusion.147
  178.7 0.9 constant_dynamic-update-slice_fusion.10
  179.6 1.4 maximum_bitcast_fusion
  181.1 2.1 collective-permute-start.4
  183.2 4.8 %collective-permute-start.7 = (bf16[1,256,512]{1,2,0:T(8,128)(2,1)S(1)}, bf16[1,256,512]{1,2,0:T(8,128)(2,1)S(1)}, u32[]{:S(2)}, u32[]{:S(2)}) collective-permute-start(bf16[1,256,512]{1,2,0:T(8,128)(2,1)S(1)} %get-tuple-element.146), channel_id=1, source_target_pairs={{16,0},{20,4},{24,8},{28,12},{32,16},{36,20},{40,24},{44,28},{48,3... | collective-permute-start | bytes 786440 | tf_op jit(solution)/shard_map/ppermute | solution.py:21
  188.0 3.3 %collective-permute-start.6 = (bf16[1,256,512]{1,2,0:T(8,128)(2,1)S(1)}, bf16[1,256,512]{1,2,0:T(8,128)(2,1)S(1)}, u32[]{:S(2)}, u32[]{:S(2)}) collective-permute-start(bf16[1,256,512]{1,2,0:T(8,128)(2,1)S(1)} %get-tuple-element.147), channel_id=1, source_target_pairs={{12,0},{16,4},{20,8},{24,12},{28,16},{32,20},{36,24},{40,28},{44,3... | collective-permute-start | bytes 786440 | tf_op jit(solution)/shard_map/ppermute | solution.py:21
  191.3 2.1 collective-permute-start.5
  193.4 1.1 broadcast_select_fusion.2
  194.4 1.2 broadcast_select_fusion.3
  195.6 2.3 collective-permute-done.6
  197.9 6.9 %collective-permute-done.5 = bf16[1,256,512]{1,2,0:T(8,128)(2,1)S(1)} collective-permute-done((bf16[1,256,512]{1,2,0:T(8,128)(2,1)S(1)}, bf16[1,256,512]{1,2,0:T(8,128)(2,1)S(1)}, u32[]{:S(2)}, u32[]{:S(2)}) %collective-permute-start.5) | collective-permute-done | bytes 262176 | tf_op jit(solution)/shard_map/ppermute | solution.py:21
  205.1 1.1 collective-permute-start.9
  206.3 1.6 collective-permute-done.9
  207.9 2.9 multiply_convert_fusion
  210.9 1.9 convolution_convert_fusion.1
  212.8 2.8 pad_maximum_fusion
  215.6 14.9 %all-to-all-start = ((bf16[64,32,1280]{2,1,0:T(8,128)(2,1)}), bf16[64,32,1280]{2,1,0:T(8,128)(2,1)}, u32[]{:S(2)}, u32[]{:S(2)}) async-start(bf16[64,32,1280]{2,1,0:T(8,128)(2,1)} %pad_maximum_fusion), calls=%async_computation | async-start | bytes 10485760 | tf_op jit(solution)/shard_map/all_to_all | solution.py:181
  230.5 3.8 %fusion.96 = f32[256,2048]{1,0:T(8,128)S(1)} fusion(bf16[256,1024]{0,1:T(8,128)(2,1)} %bitcast.15, bf16[2048,1024]{1,0:T(8,128)(2,1)} %all-gather.6.cloned.1.call-done), kind=kOutput, calls=%fused_computation.144 | convolution fusion | flops 1073741824 | bytes 6815744 | tf_op jit(solution)/shard_map/sic,dc->sid/dot_general | solution.py:142
  234.4 3.5 %fusion.63 = bf16[1,256,2048]{2,1,0:T(8,128)(2,1)} fusion(bf16[256,1024]{0,1:T(8,128)(2,1)} %bitcast.12, bf16[2048,1024]{1,0:T(8,128)(2,1)S(1)} %copy-done.7, bf16[1,256,2048]{2,1,0:T(8,128)(2,1)S(1)} %copy-done.8), kind=kOutput, calls=%fused_computation.77 | convolution fusion | flops 1075838976 | bytes 6815744 | tf_op jit(solution)/shard_map/sic,dc->sid/dot_general | solution.py:140
  237.9 1.0 fusion.64
  238.9 62.1 %all-to-all-done = bf16[64,32,1280]{2,1,0:T(8,128)(2,1)} async-done(((bf16[64,32,1280]{2,1,0:T(8,128)(2,1)}), bf16[64,32,1280]{2,1,0:T(8,128)(2,1)}, u32[]{:S(2)}, u32[]{:S(2)}) %all-to-all-start) | async-done | bytes 5242912 | tf_op jit(solution)/shard_map/all_to_all | solution.py:181
  301.0 3.4 %convert_reduce_fusion = f32[32,1280]{1,0:T(8,128)S(1)} fusion(bf16[64,32,1280]{2,1,0:T(8,128)(2,1)} %all-to-all-done), kind=kLoop, calls=%fused_computation.63 | loop fusion | flops 5201920 | bytes 5406720 | tf_op jit(solution)/shard_map/reduce_sum | solution.py:182
  304.4 2.0 collective-permute-start.11
  306.4 1.6 fusion.68
  308.1 0.7 copy-done.6
  (78 shorter events, 3.3 us)
Async XLA Ops:
  7.2 3.0 copy-start
  7.2 31.1 %all-gather.4.cloned.1.call-start = ((), (), s32[]{:S(2)}) async-start(), calls=%async_computation.1 | async-start | bytes 2621440 | tf_op jit(solution)/shard_map/all_gather | solution.py:104
  7.9 77.9 %all-gather.8.cloned.1.call-start = ((), (), s32[]{:S(2)}) async-start(), calls=%async_computation.3 | async-start | bytes 5242880 | tf_op jit(solution)/shard_map/all_gather | solution.py:105
  8.7 119.2 %all-gather.6.cloned.1.call-start = ((), (), s32[]{:S(2)}) async-start(), calls=%async_computation.2 | async-start | bytes 5242880 | tf_op jit(solution)/shard_map/all_gather | solution.py:103
  9.4 196.9 %collective-permute-start.10 = (bf16[256,2048]{1,0:T(8,128)(2,1)}, bf16[256,2048]{1,0:T(8,128)(2,1)}, u32[]{:S(2)}, u32[]{:S(2)}) collective-permute-start(bf16[256,2048]{1,0:T(8,128)(2,1)} %bitcast.9), channel_id=1, source_target_pairs={{0,1},{1,0},{2,3},{3,2},{4,5},{5,4},{6,7},{7,6},{8,9},{9,8},{10,11... | collective-permute-start | bytes 3145736 | tf_op jit(solution)/shard_map/ppermute | solution.py:25
  10.7 117.2 %copy-start.4 = (bf16[256,2048]{1,0:T(8,128)(2,1)}, bf16[256,2048]{1,0:T(8,128)(2,1)S(1)}, u32[]{:S(2)}) copy-start(bf16[256,2048]{1,0:T(8,128)(2,1)S(1)} %fusion.78) | copy-start | bytes 3145732
  40.6 17.3 %collective-permute-start = (bf16[1,256,512]{2,1,0:T(8,128)(2,1)S(1)}, bf16[1,256,512]{2,1,0:T(8,128)(2,1)S(1)}, u32[]{:S(2)}, u32[]{:S(2)}) collective-permute-start(bf16[1,256,512]{2,1,0:T(8,128)(2,1)S(1)} %fusion.77), channel_id=1, source_target_pairs={{0,16},{4,20},{8,24},{12,28},{16,32},{20,36},{24,40},{28,44},{32,4... | collective-permute-start | bytes 786440 | tf_op jit(solution)/shard_map/ppermute | solution.py:21
  41.9 16.0 %collective-permute-start.1 = (bf16[1,256,512]{2,1,0:T(8,128)(2,1)S(1)}, bf16[1,256,512]{2,1,0:T(8,128)(2,1)S(1)}, u32[]{:S(2)}, u32[]{:S(2)}) collective-permute-start(bf16[1,256,512]{2,1,0:T(8,128)(2,1)S(1)} %fusion.77), channel_id=1, source_target_pairs={{0,12},{4,16},{8,20},{12,24},{16,28},{20,32},{24,36},{28,40},{32,4... | collective-permute-start | bytes 786440 | tf_op jit(solution)/shard_map/ppermute | solution.py:21
  44.8 24.4 %collective-permute-start.2 = (bf16[1,256,512]{2,1,0:T(8,128)(2,1)S(1)}, bf16[1,256,512]{2,1,0:T(8,128)(2,1)S(1)}, u32[]{:S(2)}, u32[]{:S(2)}) collective-permute-start(bf16[1,256,512]{2,1,0:T(8,128)(2,1)S(1)} %fusion.77), channel_id=1, source_target_pairs={{0,8},{4,12},{8,16},{12,20},{16,24},{20,28},{24,32},{28,36},{32,40... | collective-permute-start | bytes 786440 | tf_op jit(solution)/shard_map/ppermute | solution.py:21
  46.8 22.4 %collective-permute-start.3 = (bf16[1,256,512]{2,1,0:T(8,128)(2,1)S(1)}, bf16[1,256,512]{2,1,0:T(8,128)(2,1)S(1)}, u32[]{:S(2)}, u32[]{:S(2)}) collective-permute-start(bf16[1,256,512]{2,1,0:T(8,128)(2,1)S(1)} %fusion.77), channel_id=1, source_target_pairs={{0,4},{4,8},{8,12},{12,16},{16,20},{20,24},{24,28},{28,32},{32,36}... | collective-permute-start | bytes 786440 | tf_op jit(solution)/shard_map/ppermute | solution.py:21
  140.2 8.2 %slice-start = ((s8[5242880]{0:T(1024)(128)(4,1)}), s8[4194304]{0:T(1024)(128)(4,1)S(1)}, s32[]{:S(2)}) async-start(s8[5242880]{0:T(1024)(128)(4,1)} %bitcast.206), calls=%async_computation.4 | async-start | bytes 8388608 | tf_op jit(solution)/shard_map/while/body/eval_jaxpr/while
  144.2 4.2 %slice-start.1 = ((s8[5242880]{0:T(1024)(128)(4,1)}), s8[1048576]{0:T(1024)(128)(4,1)S(1)}, s32[]{:S(2)}) async-start(s8[5242880]{0:T(1024)(128)(4,1)} %bitcast.206), calls=%async_computation.5 | async-start | bytes 2097152 | tf_op jit(solution)/shard_map/while/body/eval_jaxpr/while
  163.6 8.2 %slice-start = ((s8[5242880]{0:T(1024)(128)(4,1)}), s8[4194304]{0:T(1024)(128)(4,1)S(1)}, s32[]{:S(2)}) async-start(s8[5242880]{0:T(1024)(128)(4,1)} %bitcast.206), calls=%async_computation.4 | async-start | bytes 8388608 | tf_op jit(solution)/shard_map/while/body/eval_jaxpr/while
  167.6 4.2 %slice-start.1 = ((s8[5242880]{0:T(1024)(128)(4,1)}), s8[1048576]{0:T(1024)(128)(4,1)S(1)}, s32[]{:S(2)}) async-start(s8[5242880]{0:T(1024)(128)(4,1)} %bitcast.206), calls=%async_computation.5 | async-start | bytes 2097152 | tf_op jit(solution)/shard_map/while/body/eval_jaxpr/while
  181.1 14.5 %collective-permute-start.4 = (bf16[1,256,512]{1,2,0:T(8,128)(2,1)S(1)}, bf16[1,256,512]{1,2,0:T(8,128)(2,1)S(1)}, u32[]{:S(2)}, u32[]{:S(2)}) collective-permute-start(bf16[1,256,512]{1,2,0:T(8,128)(2,1)S(1)} %get-tuple-element.145), channel_id=1, source_target_pairs={{4,0},{8,4},{12,8},{16,12},{20,16},{24,20},{28,24},{32,28},{36,32}... | collective-permute-start | bytes 786440 | tf_op jit(solution)/shard_map/ppermute | solution.py:21
  183.2 12.4 %collective-permute-start.7 = (bf16[1,256,512]{1,2,0:T(8,128)(2,1)S(1)}, bf16[1,256,512]{1,2,0:T(8,128)(2,1)S(1)}, u32[]{:S(2)}, u32[]{:S(2)}) collective-permute-start(bf16[1,256,512]{1,2,0:T(8,128)(2,1)S(1)} %get-tuple-element.146), channel_id=1, source_target_pairs={{16,0},{20,4},{24,8},{28,12},{32,16},{36,20},{40,24},{44,28},{48,3... | collective-permute-start | bytes 786440 | tf_op jit(solution)/shard_map/ppermute | solution.py:21
  188.0 9.9 %collective-permute-start.6 = (bf16[1,256,512]{1,2,0:T(8,128)(2,1)S(1)}, bf16[1,256,512]{1,2,0:T(8,128)(2,1)S(1)}, u32[]{:S(2)}, u32[]{:S(2)}) collective-permute-start(bf16[1,256,512]{1,2,0:T(8,128)(2,1)S(1)} %get-tuple-element.147), channel_id=1, source_target_pairs={{12,0},{16,4},{20,8},{24,12},{28,16},{32,20},{36,24},{40,28},{44,3... | collective-permute-start | bytes 786440 | tf_op jit(solution)/shard_map/ppermute | solution.py:21
  191.3 13.6 %collective-permute-start.5 = (bf16[1,256,512]{1,2,0:T(8,128)(2,1)S(1)}, bf16[1,256,512]{1,2,0:T(8,128)(2,1)S(1)}, u32[]{:S(2)}, u32[]{:S(2)}) collective-permute-start(bf16[1,256,512]{1,2,0:T(8,128)(2,1)S(1)} %get-tuple-element.148), channel_id=1, source_target_pairs={{8,0},{12,4},{16,8},{20,12},{24,16},{28,20},{32,24},{36,28},{40,32... | collective-permute-start | bytes 786440 | tf_op jit(solution)/shard_map/ppermute | solution.py:21
  194.4 11.8 %copy-start.5 = (bf16[256,2048]{1,0:T(8,128)(2,1)S(1)}, bf16[256,2048]{1,0:T(8,128)(2,1)}, u32[]{:S(2)}) copy-start(bf16[256,2048]{1,0:T(8,128)(2,1)} %copy-done.4) | copy-start | bytes 3145732
  205.1 2.9 collective-permute-start.9
  206.2 4.7 %collective-permute-start.8 = (bf16[256,2048]{1,0:T(8,128)(2,1)S(1)}, bf16[256,2048]{1,0:T(8,128)(2,1)S(1)}, u32[]{:S(2)}, u32[]{:S(2)}) collective-permute-start(bf16[256,2048]{1,0:T(8,128)(2,1)S(1)} %copy-done.5), channel_id=1, source_target_pairs={{0,1},{1,0},{2,3},{3,2},{4,5},{5,4},{6,7},{7,6},{8,9},{9,8},{10,11... | collective-permute-start | bytes 3145736 | tf_op jit(solution)/shard_map/ppermute | solution.py:25
  215.6 85.4 %all-to-all-start = ((bf16[64,32,1280]{2,1,0:T(8,128)(2,1)}), bf16[64,32,1280]{2,1,0:T(8,128)(2,1)}, u32[]{:S(2)}, u32[]{:S(2)}) async-start(bf16[64,32,1280]{2,1,0:T(8,128)(2,1)} %pad_maximum_fusion), calls=%async_computation | async-start | bytes 10485760 | tf_op jit(solution)/shard_map/all_to_all | solution.py:181
  230.5 3.8 %copy-start.7 = (bf16[2048,1024]{1,0:T(8,128)(2,1)S(1)}, bf16[2048,1024]{1,0:T(8,128)(2,1)}, u32[]{:S(2)}) copy-start(bf16[2048,1024]{1,0:T(8,128)(2,1)} %all-gather.8.cloned.1.call-done) | copy-start | bytes 12582916
  230.5 3.9 %copy-start.8 = (bf16[1,256,2048]{2,1,0:T(8,128)(2,1)S(1)}, bf16[1,256,2048]{2,1,0:T(8,128)(2,1)}, u32[]{:S(2)}) copy-start(bf16[1,256,2048]{2,1,0:T(8,128)(2,1)} %param.10) | copy-start | bytes 3145732
  234.4 3.5 %copy-start.1 = (bf16[1,256,2048]{2,1,0:T(8,128)(2,1)S(1)}, bf16[1,256,2048]{2,1,0:T(8,128)(2,1)}, u32[]{:S(2)}) copy-start(bf16[1,256,2048]{2,1,0:T(8,128)(2,1)} %param.9) | copy-start | bytes 3145732
  234.4 3.5 %copy-start.2 = (bf16[2048,512]{1,0:T(8,128)(2,1)S(1)}, bf16[2048,512]{1,0:T(8,128)(2,1)}, u32[]{:S(2)}) copy-start(bf16[2048,512]{1,0:T(8,128)(2,1)} %all-gather.4.cloned.1.call-done) | copy-start | bytes 6291460
  301.0 5.4 %copy-start.3 = (bf16[1,256,2048]{2,1,0:T(8,128)(2,1)S(1)}, bf16[1,256,2048]{2,1,0:T(8,128)(2,1)}, u32[]{:S(2)}) copy-start(bf16[1,256,2048]{2,1,0:T(8,128)(2,1)} %param.11) | copy-start | bytes 3145732
  304.4 3.6 %collective-permute-start.11 = (f32[16,1280]{1,0:T(8,128)S(1)}, f32[16,1280]{1,0:T(8,128)S(1)}, u32[]{:S(2)}, u32[]{:S(2)}) collective-permute-start(f32[16,1280]{1,0:T(8,128)S(1)} %slice_select_fusion), channel_id=1, source_target_pairs={{0,1},{1,0},{2,3},{3,2},{4,5},{5,4},{6,7},{7,6},{8,9},{9,8},{10,11... | collective-permute-start | bytes 245768 | tf_op jit(solution)/shard_map/ppermute | solution.py:25
  308.1 0.7 copy-start.6
Sparse Core Ops, SparseCore 0:
  9.7 28.5 all-gather.3
  39.9 45.8 all-gather.7
  87.5 40.3 all-gather.5
where the time goes:
time: 316 us; the launch traced here: 315 us
  waiting for transfers between devices  175 us (55%)
  matrix products  54.2 us (17%)
  starting transfers between devices  39.3 us (12%)
  other arithmetic  24.2 us (8%)
  between operations  14.2 us (4%)
  local copies, waits for them, and re-layouts  7.93 us (3%)
    all_to_all x1, waiting for transfers between devices, shards(): terms = lax.all_to_all(terms, CHIPS, 0, 0)  62.1 us
    all_gather x1, waiting for transfers between devices, shards(): lax.all_gather(w_q, FSDP, axis=0, tiled=True)  37.9 us
    ppermute x8, waiting for transfers between devices, from_behind(): lax.ppermute(value, axis, [(source, source + steps) for source in range(l...  29.6 us
    all_gather x1, waiting for transfers between devices, shards(): lax.all_gather(w_kv, FSDP, axis=0, tiled=True)  27.6 us
    ppermute x8, starting transfers between devices, from_behind(): lax.ppermute(value, axis, [(source, source + steps) for source in range(l...  20.3 us
    all_to_all x1, starting transfers between devices, shards(): terms = lax.all_to_all(terms, CHIPS, 0, 0)  14.9 us
    all_gather x1, waiting for transfers between devices, shards(): lax.all_gather(w_out, FSDP, axis=0, tiled=True)  14.4 us
    sub x2, matrix products, head_block(): expo = jnp.exp(scores - top)  10.4 us
  transfers between devices with their start and end apart: 16, of which 9 were waited for; matrix products, arithmetic and copies ran while one was open for 25% of the time, Pallas kernels for 0%

commit v1 on v0

--- a/solution.py
+++ b/solution.py
@@ -13,6 +13,15 @@
 CTX = ("x", "z", "yl")
 FSDP = ("yh", "c")
 CHIPS = ("x", "z", "yl", "yh")
+settle_copies = lambda field: jnp.concatenate(
+    lax.all_to_all(
+        jnp.stack([field] * lax.psum(1, axis_name=FSDP), axis=0),
+        axis_name=FSDP,
+        concat_axis=0,
+        split_axis=0,
+    ),
+    axis=0,
+)
 
 
 def from_behind(value, axis, steps):
@@ -100,7 +109,7 @@
 
 def shards(x_cur, x_next, cot_cur, cot_next, w_q, w_kv, w_out):
     full_q, full_kv, full_out = (
-        lax.all_gather(w_q, FSDP, axis=0, tiled=True),
+        settle_copies(w_q),
         lax.all_gather(w_kv, FSDP, axis=0, tiled=True),
         lax.all_gather(w_out, FSDP, axis=0, tiled=True),
     )

time: 316 us -> 317 us (level)
  waiting for transfers between devices: 175 us -> 151 us
  starting transfers between devices: 39.3 us -> 56.1 us
  local copies, waits for them, and re-layouts: 7.93 us -> 16.4 us
    all_gather x1 -> x0, waiting for transfers between devices: 37.9 us -> none  [shards(): lax.all_gather(w_q, FSDP, axis=0, tiled=True)]
    all_to_all x0 -> x1, waiting for transfers between devices: none -> 28.2 us  [lax.all_to_all(jnp.stack([field] * lax.psum(1, axis_name=FSDP), axis=0),...]
    all_gather x1, waiting for transfers between devices: 14.4 us -> 2.48 us  [shards(): lax.all_gather(w_out, FSDP, axis=0, tiled=True)]
    all_to_all x1, starting transfers between devices: 14.9 us -> 24.6 us  [shards(): terms = lax.all_to_all(terms, CHIPS, 0, 0)]
    ppermute x8, waiting for transfers between devices: 29.6 us -> 21.6 us  [from_behind(): lax.ppermute(value, axis, [(source, source + steps) for source in range(l...]
    while x10 -> x38, local copies, waits for them, and re-layouts: 0.41 us -> 7.12 us
    all_to_all x0 -> x1, starting transfers between devices: none -> 5.58 us  [lax.all_to_all(jnp.stack([field] * lax.psum(1, axis_name=FSDP), axis=0),...]
    all_gather x1, waiting for transfers between devices: 27.6 us -> 32.1 us  [shards(): lax.all_gather(w_kv, FSDP, axis=0, tiled=True)]
  transfers between devices with their start and end apart: 16 -> 16, of which waited for: 9 -> 8; matrix products, arithmetic and copies ran while one was open for 25% -> 26% of each run, Pallas kernels for 0% -> 0%
where the time goes in v1:
time: 317 us; the launch traced here: 316 us
  waiting for transfers between devices  151 us (48%)
  starting transfers between devices  56.1 us (18%)
  matrix products  54.2 us (17%)
  other arithmetic  23.7 us (7%)
  local copies, waits for them, and re-layouts  16.4 us (5%)
  between operations  14.5 us (5%)
    all_to_all x1, waiting for transfers between devices, shards(): terms = lax.all_to_all(terms, CHIPS, 0, 0)  63.5 us
    all_gather x1, waiting for transfers between devices, shards(): lax.all_gather(w_kv, FSDP, axis=0, tiled=True)  32.1 us
    all_to_all x1, waiting for transfers between devices, lax.all_to_all(jnp.stack([field] * lax.psum(1, axis_name=FSDP), axis=0),...  28.2 us
    all_to_all x1, starting transfers between devices, shards(): terms = lax.all_to_all(terms, CHIPS, 0, 0)  24.6 us
    ppermute x8, waiting for transfers between devices, from_behind(): lax.ppermute(value, axis, [(source, source + steps) for source in range(l...  21.6 us
    ppermute x8, starting transfers between devices, from_behind(): lax.ppermute(value, axis, [(source, source + steps) for source in range(l...  21.4 us
    sub x2, matrix products, head_block(): expo = jnp.exp(scores - top)  10.1 us
    dot_general x2, matrix products, head_block(): jnp.einsum('imd,jd->mij', grad3, vals2, preferred_element_type=jnp.float32)  8.12 us
  transfers between devices with their start and end apart: 16, of which 8 were waited for; matrix products, arithmetic and copies ran while one was open for 26% of the time, Pallas kernels for 0%

profile of v1, /device:TPU:71, one launch (start us, length us, event | category | flops | bytes accessed | tf_op | source)
XLA Modules:
  0.0 316.0 jit_solution(1303570515897018591)
XLA Ops:
  8.7 2.5 stack.2
  11.2 5.6 %all-to-all-start = ((bf16[4,512,1024]{2,1,0:T(8,128)(2,1)}), bf16[4,512,1024]{2,1,0:T(8,128)(2,1)}, u32[]{:S(2)}, u32[]{:S(2)}) async-start(bf16[4,512,1024]{2,1,0:T(8,128)(2,1)} %stack.2), calls=%async_computation | async-start | bytes 8388608 | tf_op jit(solution)/shard_map/all_to_all | solution.py:17
  17.5 32.1 %all-gather.3.cloned.1.call-done = bf16[2048,512]{1,0:T(8,128)(2,1)} async-done(((bf16[512,512]{1,0:T(8,128)(2,1)}), bf16[2048,512]{1,0:T(8,128)(2,1)}) %all-gather.3.cloned.1.call-update) | async-done | bytes 2097168 | tf_op jit(solution)/shard_map/all_gather | solution.py:113
  49.6 2.3 fusion.77
  51.9 1.3 collective-permute-start
  53.2 2.9 collective-permute-start.1
  56.1 1.9 collective-permute-start.2
  58.1 2.1 collective-permute-start.3
  60.2 28.2 %all-to-all-done = bf16[4,512,1024]{2,1,0:T(8,128)(2,1)} async-done(((bf16[4,512,1024]{2,1,0:T(8,128)(2,1)}), bf16[4,512,1024]{2,1,0:T(8,128)(2,1)}, u32[]{:S(2)}, u32[]{:S(2)}) %all-to-all-start) | async-done | bytes 4194336 | tf_op jit(solution)/shard_map/all_to_all | solution.py:17
  88.4 3.4 %convolution_convert_fusion.2 = bf16[256,1024]{1,0:T(8,128)(2,1)S(1)} fusion(bf16[256,2048]{1,0:T(8,128)(2,1)S(1)} %fusion.78, bf16[2048,1024]{1,0:T(8,128)(2,1)} %bitcast.8), kind=kOutput, calls=%fused_computation.94 | convolution fusion | flops 1074003968 | bytes 5767168 | tf_op jit(solution)/shard_map/sid,dc->sic/dot_general | solution.py:121
  92.2 4.9 %collective-permute-done.1 = bf16[1,256,512]{2,1,0:T(8,128)(2,1)S(1)} collective-permute-done((bf16[1,256,512]{2,1,0:T(8,128)(2,1)S(1)}, bf16[1,256,512]{2,1,0:T(8,128)(2,1)S(1)}, u32[]{:S(2)}, u32[]{:S(2)}) %collective-permute-start.1) | collective-permute-done | bytes 262176 | tf_op jit(solution)/shard_map/ppermute | solution.py:30
  97.1 11.7 %collective-permute-done.3 = bf16[1,256,512]{2,1,0:T(8,128)(2,1)S(1)} collective-permute-done((bf16[1,256,512]{2,1,0:T(8,128)(2,1)S(1)}, bf16[1,256,512]{2,1,0:T(8,128)(2,1)S(1)}, u32[]{:S(2)}, u32[]{:S(2)}) %collective-permute-start.3) | collective-permute-done | bytes 262176 | tf_op jit(solution)/shard_map/ppermute | solution.py:30
  109.3 2.5 all-gather.5.cloned.1.call-done
  111.8 4.6 %fusion.76 = bf16[256,1024]{1,0:T(8,128)(2,1)} fusion(bf16[2048,1024]{1,0:T(8,128)(2,1)} %all-gather.5.cloned.1.call-done, bf16[1,256,2048]{2,1,0:T(8,128)(2,1)} %param.12), kind=kOutput, calls=%fused_computation.93 | convolution fusion | flops 1074266112 | bytes 5767168 | tf_op jit(solution)/shard_map/sid,dc->sic/dot_general | solution.py:128
  116.4 1.4 reshape.131
  117.8 1.2 copy_bitcast_fusion
  118.9 55.6 %while.29 = (s32[]{:T(128)}, bf16[2,256,4,128]{1,3,2,0:T(8,128)(2,1)}, bf16[2,256,4,128]{1,3,2,0:T(8,128)(2,1)}, bf16[2,1280,128]{1,2,0:T(8,128)(2,1)}, bf16[2,1...) while((s32[]{:T(128)}, ...), condition=%wide.region_4.5_spmd.clone, body=%wide.region_1.4_spmd.clone.sunk | while | flops 2030305536 | bytes 71074424 | solution.py:95
  118.9 0.9 fusion.142
  119.9 5.0 %exponential_reduce_fusion.2 = (f32[4,256]{1,0:T(4,128)S(1)}, f32[4,256,1280]{1,2,0:T(8,128)}) fusion(pred[256,1280]{0,1:T(8,128)(4,1)S(1)} %fusion.142, bf16[2,1280,128]{2,1,0:T(8,128)(2,1)S(1)} %get-tuple-element.280, s32[]{:T(128)} %get-tuple-element.261, bf16[2,256,4,128]{3,1,2,0:T(8,128)(2,1)} %get-tuple-element.281), kind=kOutput, calls=%fused_computation.9.clone.1 | convolution fusion | flops 340788480 | bytes 6165504 | tf_op jit(solution)/shard_map/while/body/eval_jaxpr/while/body/eval_jaxpr/sub | solution.py:49
  124.9 3.9 %fusion.143 = bf16[4,256,1280]{1,2,0:T(8,128)(2,1)S(1)} fusion(f32[4,256]{1,0:T(4,128)S(1)} %get-tuple-element.242, f32[4,256,1280]{1,2,0:T(8,128)} %get-tuple-element.243), kind=kLoop, calls=%fused_computation.18.clone.1 | loop fusion | flops 2621440 | bytes 7868416 | tf_op jit(solution)/shard_map/while/body/eval_jaxpr/while/body/eval_jaxpr/convert_element_type | solution.py:51
  128.8 1.3 fusion.144
  130.2 0.8 copy-done.14
  131.0 0.8 bitcast_convert_fusion.3
  131.8 1.2 copy.53
  133.1 1.1 fusion.145
  134.2 4.1 %fusion.146 = bf16[4,256,1280]{1,2,0:T(8,128)(2,1)S(1)} fusion(f32[4,256]{1,0:T(4,128)S(1)} %fusion.145, f32[4,256]{1,0:T(4,128)S(1)} %get-tuple-element.242, f32[4,256,1280]{1,2,0:T(8,128)} %get-tuple-element.243, bf16[2,1280,128]{1,2,0:T(8,128)(2,1)} %copy-done.5, s32[]{:T(128)} %get-tuple-element.261, bf16[2,256,4,128]{3,1,2,0:T(8,128)(2,1)} %get-tuple-element.282), kind=kOutput, calls=%fused_computation.6.clone.1 | convolution fusion | flops 342097920 | bytes 8463360 | tf_op jit(solution)/shard_map/while/body/eval_jaxpr/while/body/eval_jaxpr/imd,jd->mij/dot_general | solution.py:53
  138.3 1.5 copy-done
  139.8 0.8 fusion.149
  140.8 1.8 fusion.148
  142.8 0.9 constant_dynamic-update-slice_fusion.10
  143.7 3.1 fusion.147
  146.8 0.9 fusion.142
  147.7 5.0 %exponential_reduce_fusion.2 = (f32[4,256]{1,0:T(4,128)S(1)}, f32[4,256,1280]{1,2,0:T(8,128)}) fusion(pred[256,1280]{0,1:T(8,128)(4,1)S(1)} %fusion.142, bf16[2,1280,128]{2,1,0:T(8,128)(2,1)S(1)} %get-tuple-element.280, s32[]{:T(128)} %get-tuple-element.261, bf16[2,256,4,128]{3,1,2,0:T(8,128)(2,1)} %get-tuple-element.281), kind=kOutput, calls=%fused_computation.9.clone.1 | convolution fusion | flops 340788480 | bytes 6165504 | tf_op jit(solution)/shard_map/while/body/eval_jaxpr/while/body/eval_jaxpr/sub | solution.py:49
  152.7 3.9 %fusion.143 = bf16[4,256,1280]{1,2,0:T(8,128)(2,1)S(1)} fusion(f32[4,256]{1,0:T(4,128)S(1)} %get-tuple-element.242, f32[4,256,1280]{1,2,0:T(8,128)} %get-tuple-element.243), kind=kLoop, calls=%fused_computation.18.clone.1 | loop fusion | flops 2621440 | bytes 7868416 | tf_op jit(solution)/shard_map/while/body/eval_jaxpr/while/body/eval_jaxpr/convert_element_type | solution.py:51
  156.7 1.3 fusion.144
  158.0 0.8 copy-done.14
  158.8 0.8 bitcast_convert_fusion.3
  159.6 1.2 copy.53
  160.9 1.1 fusion.145
  162.0 4.1 %fusion.146 = bf16[4,256,1280]{1,2,0:T(8,128)(2,1)S(1)} fusion(f32[4,256]{1,0:T(4,128)S(1)} %fusion.145, f32[4,256]{1,0:T(4,128)S(1)} %get-tuple-element.242, f32[4,256,1280]{1,2,0:T(8,128)} %get-tuple-element.243, bf16[2,1280,128]{1,2,0:T(8,128)(2,1)} %copy-done.5, s32[]{:T(128)} %get-tuple-element.261, bf16[2,256,4,128]{3,1,2,0:T(8,128)(2,1)} %get-tuple-element.282), kind=kOutput, calls=%fused_computation.6.clone.1 | convolution fusion | flops 342097920 | bytes 8463360 | tf_op jit(solution)/shard_map/while/body/eval_jaxpr/while/body/eval_jaxpr/imd,jd->mij/dot_general | solution.py:53
  166.1 1.5 copy-done
  167.6 0.8 fusion.149
  168.6 1.8 fusion.148
  170.6 0.9 constant_dynamic-update-slice_fusion.10
  171.5 3.0 fusion.147
  174.6 1.4 maximum_bitcast_fusion
  176.1 2.3 collective-permute-start.4
  178.3 2.1 collective-permute-start.5
  180.4 7.0 %collective-permute-start.6 = (bf16[1,256,512]{1,2,0:T(8,128)(2,1)S(1)}, bf16[1,256,512]{1,2,0:T(8,128)(2,1)S(1)}, u32[]{:S(2)}, u32[]{:S(2)}) collective-permute-start(bf16[1,256,512]{1,2,0:T(8,128)(2,1)S(1)} %get-tuple-element.147), channel_id=1, source_target_pairs={{12,0},{16,4},{20,8},{24,12},{28,16},{32,20},{36,24},{40,28},{44,3... | collective-permute-start | bytes 786440 | tf_op jit(solution)/shard_map/ppermute | solution.py:30
  187.4 1.9 collective-permute-start.7
  189.5 5.1 %collective-permute-done.5 = bf16[1,256,512]{1,2,0:T(8,128)(2,1)S(1)} collective-permute-done((bf16[1,256,512]{1,2,0:T(8,128)(2,1)S(1)}, bf16[1,256,512]{1,2,0:T(8,128)(2,1)S(1)}, u32[]{:S(2)}, u32[]{:S(2)}) %collective-permute-start.5) | collective-permute-done | bytes 262176 | tf_op jit(solution)/shard_map/ppermute | solution.py:30
  194.8 2.1 collective-permute-start.9
  197.0 1.6 collective-permute-done.9
  198.7 2.9 multiply_convert_fusion
  201.6 1.9 convolution_convert_fusion.1
  203.5 2.7 pad_maximum_fusion
  206.2 24.6 %all-to-all-start.1 = ((bf16[64,32,1280]{2,1,0:T(8,128)(2,1)}), bf16[64,32,1280]{2,1,0:T(8,128)(2,1)}, u32[]{:S(2)}, u32[]{:S(2)}) async-start(bf16[64,32,1280]{2,1,0:T(8,128)(2,1)} %pad_maximum_fusion), calls=%async_computation.1 | async-start | bytes 10485760 | tf_op jit(solution)/shard_map/all_to_all | solution.py:190
  230.8 3.6 %fusion.96 = f32[256,2048]{1,0:T(8,128)S(1)} fusion(bf16[256,1024]{0,1:T(8,128)(2,1)S(1)} %bitcast.217, bf16[2048,1024]{1,0:T(8,128)(2,1)} %bitcast.8), kind=kOutput, calls=%fused_computation.144 | convolution fusion | flops 1073741824 | bytes 6815744 | tf_op jit(solution)/shard_map/sic,dc->sid/dot_general | solution.py:151
  234.6 2.3 fusion.63
  236.8 1.0 fusion.64
  237.9 63.5 %all-to-all-done.1 = bf16[64,32,1280]{2,1,0:T(8,128)(2,1)} async-done(((bf16[64,32,1280]{2,1,0:T(8,128)(2,1)}), bf16[64,32,1280]{2,1,0:T(8,128)(2,1)}, u32[]{:S(2)}, u32[]{:S(2)}) %all-to-all-start.1) | async-done | bytes 5242912 | tf_op jit(solution)/shard_map/all_to_all | solution.py:190
  301.4 3.4 %convert_reduce_fusion = f32[32,1280]{1,0:T(8,128)S(1)} fusion(bf16[64,32,1280]{2,1,0:T(8,128)(2,1)} %all-to-all-done.1), kind=kLoop, calls=%fused_computation.63 | loop fusion | flops 5201920 | bytes 5406720 | tf_op jit(solution)/shard_map/reduce_sum | solution.py:191
  304.8 2.0 collective-permute-start.11
  306.8 1.6 fusion.68
  (110 shorter events, 5.3 us)
Async XLA Ops:
  7.2 1.5 copy-start.9
  7.2 42.4 %all-gather.3.cloned.1.call-start = ((), (), s32[]{:S(2)}) async-start(), calls=%async_computation.2 | async-start | bytes 2621440 | tf_op jit(solution)/shard_map/all_gather | solution.py:113
  7.9 103.9 %all-gather.5.cloned.1.call-start = ((), (), s32[]{:S(2)}) async-start(), calls=%async_computation.3 | async-start | bytes 5242880 | tf_op jit(solution)/shard_map/all_gather | solution.py:114
  11.2 5.7 %copy-start.1 = (bf16[1,256,2048]{2,1,0:T(8,128)(2,1)S(1)}, bf16[1,256,2048]{2,1,0:T(8,128)(2,1)}, u32[]{:S(2)}) copy-start(bf16[1,256,2048]{2,1,0:T(8,128)(2,1)} %param.9) | copy-start | bytes 3145732
  11.2 77.2 %all-to-all-start = ((bf16[4,512,1024]{2,1,0:T(8,128)(2,1)}), bf16[4,512,1024]{2,1,0:T(8,128)(2,1)}, u32[]{:S(2)}, u32[]{:S(2)}) async-start(bf16[4,512,1024]{2,1,0:T(8,128)(2,1)} %stack.2), calls=%async_computation | async-start | bytes 8388608 | tf_op jit(solution)/shard_map/all_to_all | solution.py:17
  16.7 180.3 %collective-permute-start.10 = (bf16[256,2048]{1,0:T(8,128)(2,1)}, bf16[256,2048]{1,0:T(8,128)(2,1)}, u32[]{:S(2)}, u32[]{:S(2)}) collective-permute-start(bf16[256,2048]{1,0:T(8,128)(2,1)} %bitcast.10), channel_id=1, source_target_pairs={{0,1},{1,0},{2,3},{3,2},{4,5},{5,4},{6,7},{7,6},{8,9},{9,8},{10,11... | collective-permute-start | bytes 3145736 | tf_op jit(solution)/shard_map/ppermute | solution.py:34
  17.5 70.9 %copy-start.11 = (bf16[256,2048]{1,0:T(8,128)(2,1)}, bf16[256,2048]{1,0:T(8,128)(2,1)S(1)}, u32[]{:S(2)}) copy-start(bf16[256,2048]{1,0:T(8,128)(2,1)S(1)} %fusion.78) | copy-start | bytes 3145732
  51.9 40.3 %collective-permute-start = (bf16[1,256,512]{2,1,0:T(8,128)(2,1)S(1)}, bf16[1,256,512]{2,1,0:T(8,128)(2,1)S(1)}, u32[]{:S(2)}, u32[]{:S(2)}) collective-permute-start(bf16[1,256,512]{2,1,0:T(8,128)(2,1)S(1)} %fusion.77), channel_id=1, source_target_pairs={{0,16},{4,20},{8,24},{12,28},{16,32},{20,36},{24,40},{28,44},{32,4... | collective-permute-start | bytes 786440 | tf_op jit(solution)/shard_map/ppermute | solution.py:30
  53.2 43.9 %collective-permute-start.1 = (bf16[1,256,512]{2,1,0:T(8,128)(2,1)S(1)}, bf16[1,256,512]{2,1,0:T(8,128)(2,1)S(1)}, u32[]{:S(2)}, u32[]{:S(2)}) collective-permute-start(bf16[1,256,512]{2,1,0:T(8,128)(2,1)S(1)} %fusion.77), channel_id=1, source_target_pairs={{0,12},{4,16},{8,20},{12,24},{16,28},{20,32},{24,36},{28,40},{32,4... | collective-permute-start | bytes 786440 | tf_op jit(solution)/shard_map/ppermute | solution.py:30
  56.1 41.0 %collective-permute-start.2 = (bf16[1,256,512]{2,1,0:T(8,128)(2,1)S(1)}, bf16[1,256,512]{2,1,0:T(8,128)(2,1)S(1)}, u32[]{:S(2)}, u32[]{:S(2)}) collective-permute-start(bf16[1,256,512]{2,1,0:T(8,128)(2,1)S(1)} %fusion.77), channel_id=1, source_target_pairs={{0,8},{4,12},{8,16},{12,20},{16,24},{20,28},{24,32},{28,36},{32,40... | collective-permute-start | bytes 786440 | tf_op jit(solution)/shard_map/ppermute | solution.py:30
  58.1 50.8 %collective-permute-start.3 = (bf16[1,256,512]{2,1,0:T(8,128)(2,1)S(1)}, bf16[1,256,512]{2,1,0:T(8,128)(2,1)S(1)}, u32[]{:S(2)}, u32[]{:S(2)}) collective-permute-start(bf16[1,256,512]{2,1,0:T(8,128)(2,1)S(1)} %fusion.77), channel_id=1, source_target_pairs={{0,4},{4,8},{8,12},{12,16},{16,20},{20,24},{24,28},{28,32},{32,36}... | collective-permute-start | bytes 786440 | tf_op jit(solution)/shard_map/ppermute | solution.py:30
  118.9 6.0 %copy-start.3 = (bf16[2,1280,128]{2,1,0:T(8,128)(2,1)}, bf16[2,1280,128]{2,1,0:T(8,128)(2,1)S(1)}, u32[]{:S(2)}) copy-start(bf16[2,1280,128]{2,1,0:T(8,128)(2,1)S(1)} %get-tuple-element.280) | copy-start | bytes 1966084 | tf_op jit(solution)/shard_map/while/body/eval_jaxpr/while
  118.9 9.9 %copy-start.5 = (bf16[2,1280,128]{1,2,0:T(8,128)(2,1)}, bf16[2,1280,128]{1,2,0:T(8,128)(2,1)S(1)}, u32[]{:S(2)}) copy-start(bf16[2,1280,128]{1,2,0:T(8,128)(2,1)S(1)} %get-tuple-element.279) | copy-start | bytes 1966084 | tf_op jit(solution)/shard_map/while/body/eval_jaxpr/while
  124.9 3.9 %copy-start.13 = (bf16[2,256,4,128]{1,3,2,0:T(8,128)(2,1)S(1)}, bf16[2,256,4,128]{1,3,2,0:T(8,128)(2,1)}, u32[]{:S(2)}) copy-start(bf16[2,256,4,128]{1,3,2,0:T(8,128)(2,1)} %get-tuple-element.262) | copy-start | bytes 1572868 | tf_op jit(solution)/shard_map/while/body/eval_jaxpr/while
  128.8 2.2 copy-start.7
  130.2 0.8 copy-start.14
  134.2 5.6 %copy-start.17 = (bf16[2,256,4,128]{3,1,2,0:T(8,128)(2,1)S(1)}, bf16[2,256,4,128]{3,1,2,0:T(8,128)(2,1)}, u32[]{:S(2)}) copy-start(bf16[2,256,4,128]{3,1,2,0:T(8,128)(2,1)} %get-tuple-element.281) | copy-start | bytes 1572868 | tf_op jit(solution)/shard_map/while/body/eval_jaxpr/while
  138.3 1.5 copy-start
  142.6 1.1 copy-start.4
  143.7 3.1 copy-start.6
  146.7 6.0 %copy-start.3 = (bf16[2,1280,128]{2,1,0:T(8,128)(2,1)}, bf16[2,1280,128]{2,1,0:T(8,128)(2,1)S(1)}, u32[]{:S(2)}) copy-start(bf16[2,1280,128]{2,1,0:T(8,128)(2,1)S(1)} %get-tuple-element.280) | copy-start | bytes 1966084 | tf_op jit(solution)/shard_map/while/body/eval_jaxpr/while
  146.7 9.9 %copy-start.5 = (bf16[2,1280,128]{1,2,0:T(8,128)(2,1)}, bf16[2,1280,128]{1,2,0:T(8,128)(2,1)S(1)}, u32[]{:S(2)}) copy-start(bf16[2,1280,128]{1,2,0:T(8,128)(2,1)S(1)} %get-tuple-element.279) | copy-start | bytes 1966084 | tf_op jit(solution)/shard_map/while/body/eval_jaxpr/while
  152.7 3.9 %copy-start.13 = (bf16[2,256,4,128]{1,3,2,0:T(8,128)(2,1)S(1)}, bf16[2,256,4,128]{1,3,2,0:T(8,128)(2,1)}, u32[]{:S(2)}) copy-start(bf16[2,256,4,128]{1,3,2,0:T(8,128)(2,1)} %get-tuple-element.262) | copy-start | bytes 1572868 | tf_op jit(solution)/shard_map/while/body/eval_jaxpr/while
  156.6 2.2 copy-start.7
  158.0 0.8 copy-start.14
  162.0 5.6 %copy-start.17 = (bf16[2,256,4,128]{3,1,2,0:T(8,128)(2,1)S(1)}, bf16[2,256,4,128]{3,1,2,0:T(8,128)(2,1)}, u32[]{:S(2)}) copy-start(bf16[2,256,4,128]{3,1,2,0:T(8,128)(2,1)} %get-tuple-element.281) | copy-start | bytes 1572868 | tf_op jit(solution)/shard_map/while/body/eval_jaxpr/while
  166.1 1.5 copy-start
  170.4 1.1 copy-start.4
  171.5 3.1 copy-start.6
  174.6 14.8 %copy-start.16 = (bf16[2,256,4,128]{1,3,2,0:T(8,128)(2,1)S(1)}, bf16[2,256,4,128]{1,3,2,0:T(8,128)(2,1)}, u32[]{:S(2)}) copy-start(bf16[2,256,4,128]{1,3,2,0:T(8,128)(2,1)} %get-tuple-element.83) | copy-start | bytes 1572868
  176.0 13.4 %copy-start.15 = (bf16[2,256,4,128]{1,3,2,0:T(8,128)(2,1)S(1)}, bf16[2,256,4,128]{1,3,2,0:T(8,128)(2,1)}, u32[]{:S(2)}) copy-start(bf16[2,256,4,128]{1,3,2,0:T(8,128)(2,1)} %get-tuple-element.82) | copy-start | bytes 1572868
  176.1 13.4 %collective-permute-start.4 = (bf16[1,256,512]{1,2,0:T(8,128)(2,1)S(1)}, bf16[1,256,512]{1,2,0:T(8,128)(2,1)S(1)}, u32[]{:S(2)}, u32[]{:S(2)}) collective-permute-start(bf16[1,256,512]{1,2,0:T(8,128)(2,1)S(1)} %get-tuple-element.145), channel_id=1, source_target_pairs={{4,0},{8,4},{12,8},{16,12},{20,16},{24,20},{28,24},{32,28},{36,32}... | collective-permute-start | bytes 786440 | tf_op jit(solution)/shard_map/ppermute | solution.py:30
  178.3 16.2 %collective-permute-start.5 = (bf16[1,256,512]{1,2,0:T(8,128)(2,1)S(1)}, bf16[1,256,512]{1,2,0:T(8,128)(2,1)S(1)}, u32[]{:S(2)}, u32[]{:S(2)}) collective-permute-start(bf16[1,256,512]{1,2,0:T(8,128)(2,1)S(1)} %get-tuple-element.148), channel_id=1, source_target_pairs={{8,0},{12,4},{16,8},{20,12},{24,16},{28,20},{32,24},{36,28},{40,32... | collective-permute-start | bytes 786440 | tf_op jit(solution)/shard_map/ppermute | solution.py:30
  180.4 14.1 %collective-permute-start.6 = (bf16[1,256,512]{1,2,0:T(8,128)(2,1)S(1)}, bf16[1,256,512]{1,2,0:T(8,128)(2,1)S(1)}, u32[]{:S(2)}, u32[]{:S(2)}) collective-permute-start(bf16[1,256,512]{1,2,0:T(8,128)(2,1)S(1)} %get-tuple-element.147), channel_id=1, source_target_pairs={{12,0},{16,4},{20,8},{24,12},{28,16},{32,20},{36,24},{40,28},{44,3... | collective-permute-start | bytes 786440 | tf_op jit(solution)/shard_map/ppermute | solution.py:30
  187.4 7.1 %collective-permute-start.7 = (bf16[1,256,512]{1,2,0:T(8,128)(2,1)S(1)}, bf16[1,256,512]{1,2,0:T(8,128)(2,1)S(1)}, u32[]{:S(2)}, u32[]{:S(2)}) collective-permute-start(bf16[1,256,512]{1,2,0:T(8,128)(2,1)S(1)} %get-tuple-element.146), channel_id=1, source_target_pairs={{16,0},{20,4},{24,8},{28,12},{32,16},{36,20},{40,24},{44,28},{48,3... | collective-permute-start | bytes 786440 | tf_op jit(solution)/shard_map/ppermute | solution.py:30
  189.4 7.5 %copy-start.12 = (bf16[256,2048]{1,0:T(8,128)(2,1)S(1)}, bf16[256,2048]{1,0:T(8,128)(2,1)}, u32[]{:S(2)}) copy-start(bf16[256,2048]{1,0:T(8,128)(2,1)} %copy-done.11) | copy-start | bytes 3145732
  194.8 3.9 %collective-permute-start.9 = (bf16[256,1280]{0,1:T(8,128)(2,1)S(1)}, bf16[256,1280]{0,1:T(8,128)(2,1)S(1)}, u32[]{:S(2)}, u32[]{:S(2)}) collective-permute-start(bf16[256,1280]{0,1:T(8,128)(2,1)S(1)} %pad_maximum_fusion.2), channel_id=1, source_target_pairs={{0,1},{1,0},{2,3},{3,2},{4,5},{5,4},{6,7},{7,6},{8,9},{9,8},{10,11... | collective-permute-start | bytes 1966088 | tf_op jit(solution)/shard_map/ppermute | solution.py:34
  196.9 4.7 %collective-permute-start.8 = (bf16[256,2048]{1,0:T(8,128)(2,1)S(1)}, bf16[256,2048]{1,0:T(8,128)(2,1)S(1)}, u32[]{:S(2)}, u32[]{:S(2)}) collective-permute-start(bf16[256,2048]{1,0:T(8,128)(2,1)S(1)} %copy-done.12), channel_id=1, source_target_pairs={{0,1},{1,0},{2,3},{3,2},{4,5},{5,4},{6,7},{7,6},{8,9},{9,8},{10,11... | collective-permute-start | bytes 3145736 | tf_op jit(solution)/shard_map/ppermute | solution.py:34
  206.2 95.2 %all-to-all-start.1 = ((bf16[64,32,1280]{2,1,0:T(8,128)(2,1)}), bf16[64,32,1280]{2,1,0:T(8,128)(2,1)}, u32[]{:S(2)}, u32[]{:S(2)}) async-start(bf16[64,32,1280]{2,1,0:T(8,128)(2,1)} %pad_maximum_fusion), calls=%async_computation.1 | async-start | bytes 10485760 | tf_op jit(solution)/shard_map/all_to_all | solution.py:190
  230.8 3.7 %copy-start.19 = (bf16[2048,1024]{1,0:T(8,128)(2,1)S(1)}, bf16[2048,1024]{1,0:T(8,128)(2,1)}, u32[]{:S(2)}) copy-start(bf16[2048,1024]{1,0:T(8,128)(2,1)} %all-gather.5.cloned.1.call-done) | copy-start | bytes 12582916
  230.8 3.7 %copy-start.20 = (bf16[1,256,2048]{2,1,0:T(8,128)(2,1)S(1)}, bf16[1,256,2048]{2,1,0:T(8,128)(2,1)}, u32[]{:S(2)}) copy-start(bf16[1,256,2048]{2,1,0:T(8,128)(2,1)} %param.10) | copy-start | bytes 3145732
  234.6 2.3 copy-start.2
  234.6 2.3 copy-start.8
  301.4 5.4 %copy-start.10 = (bf16[1,256,2048]{2,1,0:T(8,128)(2,1)S(1)}, bf16[1,256,2048]{2,1,0:T(8,128)(2,1)}, u32[]{:S(2)}) copy-start(bf16[1,256,2048]{2,1,0:T(8,128)(2,1)} %param.11) | copy-start | bytes 3145732
  304.8 3.6 %collective-permute-start.11 = (f32[16,1280]{1,0:T(8,128)S(1)}, f32[16,1280]{1,0:T(8,128)S(1)}, u32[]{:S(2)}, u32[]{:S(2)}) collective-permute-start(f32[16,1280]{1,0:T(8,128)S(1)} %slice_select_fusion), channel_id=1, source_target_pairs={{0,1},{1,0},{2,3},{3,2},{4,5},{5,4},{6,7},{7,6},{8,9},{9,8},{10,11... | collective-permute-start | bytes 245768 | tf_op jit(solution)/shard_map/ppermute | solution.py:34
  308.5 0.7 copy-start.18
Sparse Core Ops, SparseCore 0:
  9.7 39.9 all-gather.2
  51.3 60.4 all-gather.4
